TPU v7x, 32 devices: a whole 2x2x4 slice. The times are simulated.
32 devices in a mesh: row: 8 (over z, y), col: 4 (over x, core).
Axes of the slice: x: 2, y: 2, z: 4, core: 2. Of those that a mesh axis runs over, the one named last changes fastest.
Arguments:
- image_states: bfloat16 [64, 3072], P(('row', 'col')), may hold values from -6 to 6
- latent: float32 [64, 64], P(('row', 'col')), may hold values from -6 to 6
- text_keys: bfloat16 [1024, 3072], P('row', 'col')
- text_values: bfloat16 [1024, 3072], P('row', 'col'), may hold values from -6 to 6
- mod_table: float32 [4, 8, 3072], replicated, may hold values from -3 to 3
- timestep: int32 [4], replicated, may hold values from 0 to 3
- grid_size: int32 [4, 2], replicated, may hold values from 1 to 8, as said below
- rope_offset: int32 [4, 2], replicated, may hold values from 0 to 63
- w_qkv: bfloat16 [3072, 9216], P(None, 'row'), may hold values from -0.109375 to 0.109375
- q_gain: float32 [128], replicated, may hold values from 0.1 to 1.9
- k_gain: float32 [128], replicated, may hold values from 0.5 to 4
- w_out: bfloat16 [3072, 3072], P('col', 'row'), may hold values from -0.109375 to 0.109375
- w_fc1: bfloat16 [3072, 12288], P(None, 'row'), may hold values from -0.109375 to 0.109375
- w_fc2: bfloat16 [12288, 3072], P('row'), may hold values from -0.0546875 to 0.0546875
- w_final: bfloat16 [3072, 64], replicated, may hold values from -0.109375 to 0.109375
Outputs:
- velocity: float32 [64, 64], P(('row', 'col'))
- next_latent: float32 [64, 64], P(('row', 'col'))
Inputs may be any that keep to these rules, and one draw needn't show every extreme that they name: `grid_size`: column 0 is a request's grid height, at most 2; column 1 its grid width, at most 8; in every draw some request has height 2 and some request width 8.
All inputs are finite; a program needn't handle non-finite values.
Results may differ from a plain program's by a relative error of at most 0.008.
Values may be sent and summed in bfloat16 or wider, within the bound.
No kernel may reach another device: no remote copies, remote signals or barrier semaphores. Data moves between devices by JAX's collectives and lax.ppermute only.
A program may use at most 128 MiB of HBM per device.

v0:
```python
import jax
import jax.numpy as jnp
from jax import lax
from jax.sharding import PartitionSpec as P

REQ = 4
TXT = 256
STEPS = 4
eps_norm = 1e-06
blend = 0.25
mask_floor = -1e30


def with_halo(cells, sides, width):
    for axis, dim in sides:
        count = lax.axis_size(axis)
        ends = count - 1
        head = lax.slice_in_dim(cells, 0, width, axis=dim)
        tail = lax.slice_in_dim(cells, cells.shape[dim] - width, cells.shape[dim], axis=dim)
        cells = jnp.concatenate(
            [
                lax.ppermute(tail, axis, [(i, (i + 1) % count) for i in range(ends)]),
                cells,
                lax.ppermute(head, axis, [((i + 1) % count, i) for i in range(ends)]),
            ],
            axis=dim,
        )
    return cells


def layer_norm(values):
    mean_value = jnp.mean(values, -1, keepdims=True)
    centred = values - mean_value
    return centred * lax.rsqrt(jnp.mean(centred * centred, -1, keepdims=True) + eps_norm)


def modulate(values, shift_vec, scale_vec):
    return (layer_norm(values) * (1.0 + scale_vec) + shift_vec).astype(jnp.bfloat16)


def rope_tables(pos_h, pos_w, head_size):
    time_half = head_size // 16
    axis_dim = (head_size - head_size // 8) // 2
    freq_index = jnp.arange(axis_dim // 2, dtype=jnp.float32)
    frequency = 10000.0 ** (-2.0 * freq_index / axis_dim)
    angles = jnp.concatenate(
        [
            jnp.zeros((pos_h.shape[0], time_half), jnp.float32),
            pos_h[:, None] * frequency[None, :],
            pos_w[:, None] * frequency[None, :],
        ],
        1,
    )
    return (jnp.cos(angles), jnp.sin(angles))


def norm_rope(values, gain_vec, cosine_table, sine_table, head_count, head_size):
    row_total = values.shape[0]
    per_head = values.astype(jnp.float32).reshape(row_total, head_count, head_size)
    per_head = (
        per_head * lax.rsqrt(jnp.mean(per_head * per_head, -1, keepdims=True) + eps_norm) * gain_vec
    )
    paired = per_head.reshape(row_total, head_count, head_size // 2, 2)
    even_part = paired[..., 0]
    odd_part = paired[..., 1]
    cos_wide = cosine_table[:, None, :]
    sin_wide = sine_table[:, None, :]
    turned = jnp.stack(
        [even_part * cos_wide - odd_part * sin_wide, even_part * sin_wide + odd_part * cos_wide], -1
    )
    return turned.reshape(row_total, head_count * head_size).astype(jnp.bfloat16)


def on_device(
    image_states,
    latent,
    text_keys,
    text_values,
    mod_table,
    timestep,
    grid_size,
    rope_offset,
    w_qkv,
    q_gain,
    k_gain,
    w_out,
    w_fc1,
    w_fc2,
    w_final,
):
    col_total = lax.axis_size("col")
    row_pos = lax.axis_index("row")
    col_pos = lax.axis_index("col")
    tile_w = image_states.shape[0]
    width = image_states.shape[1]
    head_size = q_gain.shape[0]
    head_count = width // head_size
    local_heads = head_count // col_total
    request = row_pos % REQ
    grid_row = row_pos // REQ
    grid_col = col_pos * tile_w + jnp.arange(tile_w, dtype=jnp.int32)
    req_slots = jnp.arange(REQ, dtype=jnp.int32)
    req_onehot = req_slots == request
    limits = jnp.sum(jnp.where(req_onehot[:, None], grid_size, 0), 0)
    offsets = jnp.sum(jnp.where(req_onehot[:, None], rope_offset, 0), 0)
    step_now = jnp.sum(jnp.where(req_onehot, timestep, 0))
    token_ok = (grid_row < limits[0]) & (grid_col < limits[1])
    modulation = lax.dynamic_index_in_dim(mod_table, step_now, 0, keepdims=False)
    states = image_states.astype(jnp.float32)
    normed = modulate(states, modulation[0], modulation[1])
    joined_cols = jnp.dot(
        lax.all_gather(normed, "row", axis=0, tiled=True), w_qkv, preferred_element_type=jnp.float32
    ).astype(jnp.bfloat16)
    joined = lax.all_to_all(joined_cols, "row", split_axis=0, concat_axis=1, tiled=True)
    pos_h = jnp.zeros((tile_w,), jnp.float32) + (grid_row + offsets[0]).astype(jnp.float32)
    pos_w = (grid_col + offsets[1]).astype(jnp.float32)
    cosine_table, sine_table = rope_tables(pos_h, pos_w, head_size)
    queries = norm_rope(joined[:, :width], q_gain, cosine_table, sine_table, head_count, head_size)
    image_keys = norm_rope(
        joined[:, width : 2 * width], k_gain, cosine_table, sine_table, head_count, head_size
    )
    q_heads, k_heads, v_heads = (
        lax.all_to_all(queries, "col", split_axis=1, concat_axis=0, tiled=True),
        lax.all_to_all(image_keys, "col", split_axis=1, concat_axis=0, tiled=True),
        lax.all_to_all(joined[:, 2 * width :], "col", split_axis=1, concat_axis=0, tiled=True),
    )
    image_rows = k_heads.shape[0]
    text_rows = text_keys.shape[0]
    shard_rows = image_rows + text_rows
    q_block = q_heads.reshape(image_rows, local_heads, head_size)
    key_rows = jnp.concatenate([k_heads, text_keys], 0)
    value_rows = jnp.concatenate([v_heads, text_values], 0)
    run_max = jnp.full((image_rows, local_heads), mask_floor, jnp.float32)
    key_piece = lax.all_gather(key_rows, "row", axis=0, tiled=True)
    value_piece = lax.all_gather(value_rows, "row", axis=0, tiled=True)
    piece_rows = key_piece.shape[0]
    global_row = jnp.arange(piece_rows, dtype=jnp.int32)
    shard_id = global_row // shard_rows
    within = global_row % shard_rows
    is_image = within < image_rows
    source_col = within // tile_w
    source_cell = within % tile_w
    image_req = shard_id % REQ
    text_req = (shard_id * text_rows + within - image_rows) // TXT
    key_req = jnp.where(is_image, image_req, text_req)
    key_onehot = key_req[:, None] == req_slots[None, :]
    key_height = jnp.sum(jnp.where(key_onehot, grid_size[:, 0][None, :], 0), 1)
    key_width = jnp.sum(jnp.where(key_onehot, grid_size[:, 1][None, :], 0), 1)
    image_ok = (shard_id // REQ < key_height) & (source_col * tile_w + source_cell < key_width)
    key_ok = (key_req == request) & (jnp.logical_not(is_image) | image_ok)
    scores = jnp.einsum(
        "qhd,khd->qhk",
        q_block,
        key_piece.reshape(piece_rows, local_heads, head_size),
        preferred_element_type=jnp.float32,
    ) * head_size ** (-0.5)
    new_max = jnp.maximum(run_max, jnp.max(jnp.where(key_ok, scores, mask_floor), -1))
    weights = jnp.where(key_ok, jnp.exp(scores - new_max[..., None]), 0.0)
    new_sum = jnp.sum(weights, -1)
    new_acc = jnp.einsum(
        "qhk,khd->qhd",
        weights.astype(jnp.bfloat16),
        value_piece.reshape(piece_rows, local_heads, head_size),
        preferred_element_type=jnp.float32,
    )
    mixed = (
        (new_acc / new_sum[..., None])
        .astype(jnp.bfloat16)
        .reshape(image_rows, local_heads * head_size)
    )
    partial_out = jnp.dot(
        mixed, lax.all_gather(w_out, "row", axis=1, tiled=True), preferred_element_type=jnp.float32
    )
    attended = lax.psum_scatter(
        partial_out.astype(jnp.bfloat16), "col", scatter_dimension=0, tiled=True
    ).astype(jnp.float32)
    first_res = (states + modulation[2] * attended).astype(jnp.bfloat16)
    normed_two = modulate(first_res.astype(jnp.float32), modulation[3], modulation[4])
    all_rows = lax.all_gather(normed_two, "row", axis=0, tiled=True)
    hidden = jax.nn.gelu(
        jnp.dot(all_rows, w_fc1, preferred_element_type=jnp.float32), approximate=True
    ).astype(jnp.bfloat16)
    every_term = jnp.dot(hidden, w_fc2, preferred_element_type=jnp.float32)
    every_sum = lax.psum(every_term, "row")
    mlp_out = lax.dynamic_slice_in_dim(every_sum, row_pos * tile_w, tile_w, 0)
    second_res = first_res.astype(jnp.float32) + modulation[5] * mlp_out
    normed_three = modulate(second_res, modulation[6], modulation[7])
    raw_velocity = jnp.dot(normed_three, w_final, preferred_element_type=jnp.float32)
    masked = jnp.where(token_ok[:, None], raw_velocity, 0.0)
    padded = with_halo(masked, (("col", 0),), 1)
    left_side = padded[:-2]
    right_side = padded[2:]
    velocity = jnp.where(
        token_ok[:, None], masked + blend * (left_side + right_side - 2.0 * masked), 0.0
    )
    next_latent = latent + -1.0 / STEPS * velocity
    return (velocity, next_latent)


def solution(mesh):
    placed = (
        P(("row", "col"), None),
        P(("row", "col"), None),
        P("row", "col"),
        P("row", "col"),
        P(),
        P(),
        P(),
        P(),
        P(None, "row"),
        P(),
        P(),
        P("col", "row"),
        P(None, "row"),
        P("row", None),
        P(),
    )
    return jax.shard_map(
        on_device,
        mesh=mesh,
        in_specs=placed,
        out_specs=(P(("row", "col"), None), P(("row", "col"), None)),
        check_vma=False,
    )
```

profile of v0, /device:TPU:1, one launch (start us, length us, event | category | flops | bytes accessed | tf_op | source)
XLA Modules:
  0.0 413.6 jit_solution(1863781639350607465)
XLA Ops:
  7.2 1.3 select_reduce_fusion.5
  9.8 0.8 convert_reduce_fusion.1
  10.7 0.9 fusion.36
  12.3 2.2 dynamic-slice_add_fusion
  14.5 0.8 fusion.50
  15.3 25.6 %all-gather = bf16[8,2,3072]{2,1,0:T(2,128)(2,1)S(1)} all-gather(bf16[1,2,3072]{2,1,0:T(2,128)(2,1)S(1)} %fusion.50), channel_id=1, replica_groups=mesh['row'=8,'col'=4] {'row'}, dimensions={0}, use_global_device_ids=true | all-gather | bytes 110592 | tf_op jit(solution)/shard_map/all_gather | solution.py:112
  41.0 4.0 convolution_convert_fusion.1
  45.1 0.6 all_to_all.50
  45.7 5.0 %all-to-all-start = ((bf16[8,2,1152]{2,1,0:T(2,128)(2,1)}), bf16[8,2,1152]{2,1,0:T(2,128)(2,1)S(1)}, u32[]{:S(2)}, u32[]{:S(2)}) async-start(bf16[8,2,1152]{2,1,0:T(2,128)(2,1)} %all_to_all.50), calls=%async_computation | async-start | bytes 73728 | tf_op jit(solution)/shard_map/all_to_all | solution.py:114
  51.0 0.6 fusion.85
  52.3 0.6 add_convert_fusion.4
  53.2 0.7 mul.324
  53.9 0.7 mul.306
  54.7 1.6 all-to-all-done
  56.3 0.6 slice_convert_fusion
  56.9 1.5 reshape.266
  58.5 0.7 bitcast_reduce_fusion
  59.2 2.3 reshape.264
  61.5 0.7 add_rsqrt_fusion.1
  62.2 1.0 multiply_multiply_fusion
  63.3 5.2 %slice_multiply_fusion.5 = (f32[2,24,64,1]{3,2,1,0:T(8,128)}, f32[2,24,64,1]{3,2,1,0:T(8,128)}, f32[2,24,64,1]{3,2,1,0:T(8,128)}, f32[2,24,64,1]{3,2,1,0:T(8,128...) fusion(f32[2,24,64,2]{3,2,1,0:T(8,128)S(1)} %multiply_multiply_, ...), kind=kLoop, calls=%fused_computation.11 | loop fusion | flops 24576 | bytes 148480 | tf_op jit(solution)/shard_map/mul | solution.py:69
  68.5 2.5 copy.52
  71.1 2.5 copy.53
  73.6 2.5 copy.54
  76.1 2.5 copy.55
  78.6 0.8 subtract_convert_fusion.1
  79.4 0.8 add_convert_fusion.2
  80.2 0.6 pad_maximum_fusion.2
  80.8 2.0 copy.56
  82.8 2.1 convert_element_type.69
  84.9 14.5 %all_to_all.67 = bf16[2,4,768]{2,0,1:T(2,128)(2,1)} all-to-all(bf16[2,4,768]{2,0,1:T(2,128)(2,1)S(1)} %copy.57), channel_id=1, replica_groups=mesh['row'=8,'col'=4] {'col'}, dimensions={1} | all-to-all | bytes 24576 | tf_op jit(solution)/shard_map/all_to_all | solution.py:124
  99.4 0.7 all_to_all.60
  100.1 1.6 pad_maximum_fusion.1
  101.8 7.8 %all_to_all.68 = bf16[2,4,768]{2,0,1:T(2,128)(2,1)} all-to-all(bf16[2,4,768]{2,0,1:T(2,128)(2,1)} %bitcast.72), channel_id=1, replica_groups=mesh['row'=8,'col'=4] {'col'}, dimensions={1} | all-to-all | bytes 24576 | tf_op jit(solution)/shard_map/all_to_all | solution.py:125
  109.6 0.7 all_to_all.57
  110.3 1.6 pad_maximum_fusion
  112.0 0.7 all-gather.10.cloned.1.call-update
  112.8 2.5 copy.59
  115.4 2.5 copy.60
  117.9 1.1 copy.61
  119.0 0.5 copy.62
  119.8 0.4 copy.63
  120.2 1.1 convert_element_type.71
  121.3 0.6 copy.64
  121.9 3.9 all-to-all-start.3
  125.9 0.6 dynamic-slice
  127.2 2.2 all-to-all-done.3
  129.4 14.7 %all-gather.8.cloned.1.call-done = bf16[1088,768]{1,0:T(8,128)(2,1)} async-done(((bf16[136,768]{1,0:T(8,128)(2,1)}), bf16[1088,768]{1,0:T(8,128)(2,1)}) %all-gather.8.cloned.1.call-update) | async-done | bytes 1671184 | tf_op jit(solution)/shard_map/all_gather | solution.py:134
  144.1 3.8 copy.58
  147.9 42.3 %all-gather.6.cloned.1.call-done = bf16[1088,768]{1,0:T(8,128)(2,1)} async-done(((bf16[136,768]{1,0:T(8,128)(2,1)}), bf16[1088,768]{1,0:T(8,128)(2,1)}) %all-gather.6.cloned.1.call-update) | async-done | bytes 1671184 | tf_op jit(solution)/shard_map/all_gather | solution.py:135
  190.2 2.7 copy.51
  192.9 1.9 select_reduce_fusion
  195.0 77.3 %all-gather.10.cloned.1.call-done = bf16[768,3072]{1,0:T(8,128)(2,1)} async-done(((bf16[768,384]{1,0:T(8,128)(2,1)}), bf16[768,3072]{1,0:T(8,128)(2,1)}) %all-gather.10.cloned.1.call-update) | async-done | bytes 4718608 | tf_op jit(solution)/shard_map/all_gather | solution.py:172
  272.3 3.7 convolution_convert_fusion
  276.0 11.2 %all-reduce = bf16[8,3072]{1,0:T(8,128)(2,1)S(1)} all-reduce(bf16[8,3072]{1,0:T(8,128)(2,1)S(1)} %convolution_convert_fusion), channel_id=2, replica_groups=mesh['row'=8,'col'=4] {'col'}, use_global_device_ids=true, to_apply=%region_11.12.clone | all-reduce | flops 24576 | bytes 98304
  287.7 24.4 %all-gather.1 = bf16[8,2,3072]{2,1,0:T(2,128)(2,1)S(1)} all-gather(bf16[1,2,3072]{2,1,0:T(2,128)(2,1)S(1)} %fusion.51), channel_id=1, replica_groups=mesh['row'=8,'col'=4] {'row'}, dimensions={0}, use_global_device_ids=true | all-gather | bytes 110592 | tf_op jit(solution)/shard_map/all_gather | solution.py:179
  312.2 9.6 %fusion.22 = f32[16,3072]{1,0:T(8,128)} fusion(bf16[1536,3072]{1,0:T(8,128)(2,1)} %param.28, bf16[16,3072]{1,0:T(8,128)(2,1)S(1)} %reshape.272, bf16[3072,1536]{1,0:T(8,128)(2,1)} %param.27), kind=kOutput, calls=%fused_computation.37 | convolution fusion | flops 302211072 | bytes 19169280 | tf_op jit(solution)/shard_map/dot_general | solution.py:183
  322.4 0.7 compare_and_fusion
  323.0 71.4 %all-reduce.3.cloned.1.call-done = f32[16,3072]{1,0:T(8,128)} async-done(((f32[16,3072]{1,0:T(8,128)}), f32[16,3072]{1,0:T(8,128)}) %all-reduce.3.cloned.1.call-update) | async-done | bytes 196624 | tf_op jit(solution)/shard_map/psum | solution.py:184
  394.4 1.0 fusion.82
  396.0 5.6 %collective-permute-start = (f32[1,64]{1,0:T(1,128)S(1)}, f32[1,64]{1,0:T(1,128)S(1)}, u32[]{:S(2)}, u32[]{:S(2)}) collective-permute-start(f32[1,64]{1,0:T(1,128)S(1)} %get-tuple-element.45), channel_id=1, source_target_pairs={{0,1},{1,2},{2,3},{4,5},{5,6},{6,7},{8,9},{9,10},{10,11},{12,13},{... | collective-permute-start | bytes 776 | tf_op jit(solution)/shard_map/ppermute | solution.py:22
  401.5 1.9 collective-permute-start.1
  403.5 2.9 collective-permute-done.1
  406.4 0.6 multiply_add_fusion
  (81 shorter events, 2.6 us)
Async XLA Ops:
  7.2 388.5 %copy-start = (bf16[3072,64]{0,1:T(8,128)(2,1)S(1)}, bf16[3072,64]{0,1:T(8,128)(2,1)}, u32[]{:S(2)}) copy-start(bf16[3072,64]{0,1:T(8,128)(2,1)} %param.29) | copy-start | bytes 1179652
  41.0 9.8 %copy-start.12 = (s32[4,2]{0,1:T(2,128)S(1)}, s32[4,2]{0,1:T(2,128)}, u32[]{:S(2)}) copy-start(s32[4,2]{0,1:T(2,128)} %param.21) | copy-start | bytes 100
  41.0 9.8 %copy-start.13 = (s32[4,2]{0,1:T(2,128)S(1)}, s32[4,2]{0,1:T(2,128)}, u32[]{:S(2)}) copy-start(s32[4,2]{0,1:T(2,128)} %param.22) | copy-start | bytes 100
  41.0 12.1 %copy-start.15 = (f32[128]{0:T(128)S(1)}, f32[128]{0:T(128)}, u32[]{:S(2)}) copy-start(f32[128]{0:T(128)} %param.24) | copy-start | bytes 1540
  41.0 12.9 %copy-start.16 = (f32[128]{0:T(128)S(1)}, f32[128]{0:T(128)}, u32[]{:S(2)}) copy-start(f32[128]{0:T(128)} %param.25) | copy-start | bytes 1540
  45.7 10.6 %all-to-all-start = ((bf16[8,2,1152]{2,1,0:T(2,128)(2,1)}), bf16[8,2,1152]{2,1,0:T(2,128)(2,1)S(1)}, u32[]{:S(2)}, u32[]{:S(2)}) async-start(bf16[8,2,1152]{2,1,0:T(2,128)(2,1)} %all_to_all.50), calls=%async_computation | async-start | bytes 73728 | tf_op jit(solution)/shard_map/all_to_all | solution.py:114
  50.7 93.4 %all-gather.8.cloned.1.call-start = ((), (), s32[]{:S(2)}) async-start(), calls=%async_computation.5 | async-start | bytes 1880064 | tf_op jit(solution)/shard_map/all_gather | solution.py:134
  62.2 1.0 copy-start.2
  101.8 88.4 %all-gather.6.cloned.1.call-start = ((), (), s32[]{:S(2)}) async-start(), calls=%async_computation.4 | async-start | bytes 1880064 | tf_op jit(solution)/shard_map/all_gather | solution.py:135
  111.9 160.4 %all-gather.10.cloned.1.call-start = ((), (), s32[]{:S(2)}) async-start(), calls=%async_computation.6 | async-start | bytes 5308416 | tf_op jit(solution)/shard_map/all_gather | solution.py:172
  119.0 0.7 copy-start.3
  119.0 0.8 copy-start.4
  119.0 0.8 copy-start.5
  119.0 6.9 %copy-start.17 = (u32[32]{0:T(128)S(1)}, u32[32]{0:T(128)}, u32[]{:S(2)}) copy-start(u32[32]{0:T(128)} %constant.158) | copy-start | bytes 388
  121.9 7.5 %all-to-all-start.3 = ((bf16[2,4,768]{2,0,1:T(2,128)(2,1)}), bf16[2,4,768]{2,0,1:T(2,128)(2,1)S(1)}, u32[]{:S(2)}, u32[]{:S(2)}) async-start(bf16[2,4,768]{2,0,1:T(2,128)(2,1)} %copy.64), calls=%async_computation.3 | async-start | bytes 24576 | tf_op jit(solution)/shard_map/all_to_all | solution.py:123
  125.9 268.5 %all-reduce.3.cloned.1.call-start = ((), (), s32[]{:S(2)}) async-start(), calls=%async_computation.7 | async-start | bytes 393216 | tf_op jit(solution)/shard_map/psum | solution.py:184
  272.3 14.9 %copy-start.1 = (bf16[2,3072]{1,0:T(2,128)(2,1)S(1)}, bf16[2,3072]{1,0:T(2,128)(2,1)}, u32[]{:S(2)}) copy-start(bf16[2,3072]{1,0:T(2,128)(2,1)} %param.15) | copy-start | bytes 36868
  272.3 14.9 %copy-start.9 = (f32[1,1,3072]{2,1,0:T(1,128)S(1)}, f32[1,1,3072]{2,1,0:T(1,128)}, u32[]{:S(2)}) copy-start(f32[1,1,3072]{2,1,0:T(1,128)} %get-tuple-element.30) | copy-start | bytes 36868
  272.3 15.3 %copy-start.7 = (f32[1,1,3072]{2,1,0:T(1,128)S(1)}, f32[1,1,3072]{2,1,0:T(1,128)}, u32[]{:S(2)}) copy-start(f32[1,1,3072]{2,1,0:T(1,128)} %get-tuple-element.25) | copy-start | bytes 36868
  272.3 15.3 %copy-start.8 = (f32[1,1,3072]{2,1,0:T(1,128)S(1)}, f32[1,1,3072]{2,1,0:T(1,128)}, u32[]{:S(2)}) copy-start(f32[1,1,3072]{2,1,0:T(1,128)} %get-tuple-element.26) | copy-start | bytes 36868
  312.1 82.3 %copy-start.6 = (f32[1,1,3072]{2,1,0:T(1,128)S(1)}, f32[1,1,3072]{2,1,0:T(1,128)}, u32[]{:S(2)}) copy-start(f32[1,1,3072]{2,1,0:T(1,128)} %get-tuple-element.27) | copy-start | bytes 36868
  312.1 83.6 %copy-start.10 = (f32[1,1,3072]{2,1,0:T(1,128)S(1)}, f32[1,1,3072]{2,1,0:T(1,128)}, u32[]{:S(2)}) copy-start(f32[1,1,3072]{2,1,0:T(1,128)} %get-tuple-element.24) | copy-start | bytes 36868
  312.1 83.6 %copy-start.11 = (f32[1,1,3072]{2,1,0:T(1,128)S(1)}, f32[1,1,3072]{2,1,0:T(1,128)}, u32[]{:S(2)}) copy-start(f32[1,1,3072]{2,1,0:T(1,128)} %get-tuple-element.31) | copy-start | bytes 36868
  312.1 94.3 %copy-start.14 = (f32[2,64]{1,0:T(2,128)S(1)}, f32[2,64]{1,0:T(2,128)}, u32[]{:S(2)}) copy-start(f32[2,64]{1,0:T(2,128)} %param.16) | copy-start | bytes 1540
  396.0 7.5 %collective-permute-start = (f32[1,64]{1,0:T(1,128)S(1)}, f32[1,64]{1,0:T(1,128)S(1)}, u32[]{:S(2)}, u32[]{:S(2)}) collective-permute-start(f32[1,64]{1,0:T(1,128)S(1)} %get-tuple-element.45), channel_id=1, source_target_pairs={{0,1},{1,2},{2,3},{4,5},{5,6},{6,7},{8,9},{9,10},{10,11},{12,13},{... | collective-permute-start | bytes 776 | tf_op jit(solution)/shard_map/ppermute | solution.py:22
  401.5 4.9 %collective-permute-start.1 = (f32[1,64]{1,0:T(1,128)S(1)}, f32[1,64]{1,0:T(1,128)S(1)}, u32[]{:S(2)}, u32[]{:S(2)}) collective-permute-start(f32[1,64]{1,0:T(1,128)S(1)} %get-tuple-element.46), channel_id=1, source_target_pairs={{1,0},{2,1},{3,2},{5,4},{6,5},{7,6},{9,8},{10,9},{11,10},{13,12},{... | collective-permute-start | bytes 776 | tf_op jit(solution)/shard_map/ppermute | solution.py:24
Sparse Core Ops, SparseCore 0:
  101.9 42.1 all-gather.7
  146.3 43.8 all-gather.5
  192.3 79.9 all-gather.9
  321.9 72.4 all-reduce.2
where the time goes:
time: 415 us; the launch traced here: 414 us
  waiting for transfers between devices  213 us (51%)
  blocking collectives  83.5 us (20%)
  local copies, waits for them, and re-layouts  38.6 us (9%)
  other arithmetic  24.4 us (6%)
  matrix products  19.5 us (5%)
  between operations  18 us (4%)
  starting transfers between devices  16.5 us (4%)
    all_gather x1, waiting for transfers between devices, on_device(): lax.all_gather(w_out, 'row', axis=1, tiled=True)  77.3 us
    psum x1, waiting for transfers between devices, on_device(): every_sum = lax.psum(every_term, 'row')  71.4 us
    all_gather x1, waiting for transfers between devices, on_device(): value_piece = lax.all_gather(value_rows, 'row', axis=0, tiled=True)  42.3 us
    all_gather x1, blocking collectives, on_device(): lax.all_gather(normed, 'row', axis=0, tiled=True)  25.6 us
    all_gather x1, blocking collectives, on_device(): all_rows = lax.all_gather(normed_two, 'row', axis=0, tiled=True)  24.4 us
    all_gather x1, waiting for transfers between devices, on_device(): key_piece = lax.all_gather(key_rows, 'row', axis=0, tiled=True)  14.7 us
    all_to_all x1, blocking collectives, on_device(): lax.all_to_all(image_keys, 'col', split_axis=1, concat_axis=0, tiled=True)  14.5 us
    unnamed x1, blocking collectives  11.2 us
  transfers between devices with their start and end apart: 8, of which 7 were waited for; matrix products, arithmetic and copies ran while one was open for 6% of the time, Pallas kernels for 0%

commit v1 on v0

--- a/solution.py
+++ b/solution.py
@@ -9,6 +9,19 @@
 eps_norm = 1e-06
 blend = 0.25
 mask_floor = -1e30
+
+
+def gather_around(x, axis, dim):
+    ways = lax.axis_size(axis)
+    up = [(d, (d + 1) % ways) for d in range(ways)]
+    down = [(d, (d - 1) % ways) for d in range(ways)]
+    earlier, later = ([x], [x])
+    for _ in range(ways // 2):
+        earlier.append(lax.ppermute(earlier[-1], axis, up))
+    for _ in range((ways - 1) // 2):
+        later.append(lax.ppermute(later[-1], axis, down))
+    line = jnp.concatenate([*earlier[::-1], *later[1:]], axis=dim)
+    return jnp.roll(line, (lax.axis_index(axis) - ways // 2) * x.shape[dim], axis=dim)
 
 
 def with_halo(cells, sides, width):
@@ -132,7 +145,7 @@
     value_rows = jnp.concatenate([v_heads, text_values], 0)
     run_max = jnp.full((image_rows, local_heads), mask_floor, jnp.float32)
     key_piece = lax.all_gather(key_rows, "row", axis=0, tiled=True)
-    value_piece = lax.all_gather(value_rows, "row", axis=0, tiled=True)
+    value_piece = gather_around(value_rows, "row", 0)
     piece_rows = key_piece.shape[0]
     global_row = jnp.arange(piece_rows, dtype=jnp.int32)
     shard_id = global_row // shard_rows

time: 415 us -> 387 us (0.933)
  waiting for transfers between devices: 213 us -> 161 us
  starting transfers between devices: 16.5 us -> 38.5 us
  blocking collectives: 83.5 us -> 75.8 us
  local copies, waits for them, and re-layouts: 38.6 us -> 45.6 us
    all_gather x1 -> x0, waiting for transfers between devices: 42.3 us -> none  [on_device(): value_piece = lax.all_gather(value_rows, 'row', axis=0, tiled=True)]
    ppermute x0 -> x7, waiting for transfers between devices: none -> 16.4 us  [the longest x3 8.86 us: gather_around(): later.append(lax.ppermute(later[-1], axis, down))]
    all_gather x1, waiting for transfers between devices: 14.7 us -> 0.02 us  [on_device(): key_piece = lax.all_gather(key_rows, 'row', axis=0, tiled=True)]
    ppermute x0 -> x7, starting transfers between devices: none -> 12.2 us  [the longest x3 11 us: gather_around(): later.append(lax.ppermute(later[-1], axis, down))]
    all_gather x1, waiting for transfers between devices: 77.3 us -> 65.5 us  [on_device(): lax.all_gather(w_out, 'row', axis=1, tiled=True)]
    all_to_all x1 -> x0, blocking collectives: 7.75 us -> none  [on_device(): lax.all_to_all(joined[:, 2 * width:], 'col', split_axis=1, concat_axis=0,...]
    all_to_all x1, starting transfers between devices: 3.94 us -> 9.81 us  [on_device(): lax.all_to_all(queries, 'col', split_axis=1, concat_axis=0, tiled=True)]
    dynamic_slice x0 -> x2, local copies, waits for them, and re-layouts: none -> 4.38 us  [gather_around(): jnp.roll(line, (lax.axis_index(axis) - ways // 2) * x.shape[dim], axis=dim)]
  transfers between devices with their start and end apart: 8 -> 15, of which waited for: 7 -> 10; matrix products, arithmetic and copies ran while one was open for 6% -> 8% of each run, Pallas kernels for 0% -> 0%
where the time goes in v1:
time: 387 us; the launch traced here: 385 us
  waiting for transfers between devices  161 us (42%)
  blocking collectives  75.8 us (20%)
  local copies, waits for them, and re-layouts  45.6 us (12%)
  starting transfers between devices  38.5 us (10%)
  other arithmetic  26.2 us (7%)
  matrix products  19.5 us (5%)
  between operations  18.2 us (5%)
    psum x1, waiting for transfers between devices, on_device(): every_sum = lax.psum(every_term, 'row')  71.4 us
    all_gather x1, waiting for transfers between devices, on_device(): lax.all_gather(w_out, 'row', axis=1, tiled=True)  65.5 us
    all_gather x1, blocking collectives, on_device(): lax.all_gather(normed, 'row', axis=0, tiled=True)  25.6 us
    all_gather x1, blocking collectives, on_device(): all_rows = lax.all_gather(normed_two, 'row', axis=0, tiled=True)  24.4 us
    all_to_all x1, blocking collectives, on_device(): lax.all_to_all(image_keys, 'col', split_axis=1, concat_axis=0, tiled=True)  14.5 us
    unnamed x1, blocking collectives  11.2 us
    ppermute x3, starting transfers between devices, gather_around(): later.append(lax.ppermute(later[-1], axis, down))  11 us
    all_to_all x1, starting transfers between devices, on_device(): lax.all_to_all(queries, 'col', split_axis=1, concat_axis=0, tiled=True)  9.81 us
  transfers between devices with their start and end apart: 15, of which 10 were waited for; matrix products, arithmetic and copies ran while one was open for 8% of the time, Pallas kernels for 0%

profile of v1, /device:TPU:1, one launch (start us, length us, event | category | flops | bytes accessed | tf_op | source)
XLA Modules:
  0.0 385.3 jit_solution(2982971903917605816)
XLA Ops:
  7.2 1.3 select_reduce_fusion.5
  9.8 0.8 convert_reduce_fusion.1
  10.7 0.9 fusion.36
  12.3 2.2 dynamic-slice_add_fusion
  14.5 0.8 fusion.50
  15.3 25.6 %all-gather = bf16[8,2,3072]{2,1,0:T(2,128)(2,1)S(1)} all-gather(bf16[1,2,3072]{2,1,0:T(2,128)(2,1)S(1)} %fusion.50), channel_id=1, replica_groups=mesh['row'=8,'col'=4] {'row'}, dimensions={0}, use_global_device_ids=true | all-gather | bytes 110592 | tf_op jit(solution)/shard_map/all_gather | solution.py:125
  41.0 4.0 %convolution_convert_fusion.1 = bf16[16,1152]{1,0:T(8,128)(2,1)S(1)} fusion(bf16[16,3072]{1,0:T(8,128)(2,1)S(1)} %reshape.270, bf16[3072,1152]{1,0:T(8,128)(2,1)} %param.23), kind=kOutput, calls=%fused_computation.3 | convolution fusion | flops 113264640 | bytes 7213056 | tf_op jit(solution)/shard_map/dot_general | solution.py:124
  45.7 5.0 %all-to-all-start = ((bf16[8,2,1152]{2,1,0:T(2,128)(2,1)}), bf16[8,2,1152]{2,1,0:T(2,128)(2,1)S(1)}, u32[]{:S(2)}, u32[]{:S(2)}) async-start(bf16[8,2,1152]{2,1,0:T(2,128)(2,1)} %all_to_all.50), calls=%async_computation | async-start | bytes 73728 | tf_op jit(solution)/shard_map/all_to_all | solution.py:127
  53.2 0.7 mul.328
  53.9 0.7 mul.310
  54.7 1.6 all-to-all-done
  57.0 1.5 reshape.266
  59.2 2.3 reshape.264
  62.2 1.0 multiply_multiply_fusion
  63.1 0.9 multiply_multiply_fusion.1
  64.1 5.2 %slice_multiply_fusion.5 = (f32[2,24,64,1]{3,2,1,0:T(8,128)}, f32[2,24,64,1]{3,2,1,0:T(8,128)}, f32[2,24,64,1]{3,2,1,0:T(8,128)}, f32[2,24,64,1]{3,2,1,0:T(8,128...) fusion(f32[2,24,64,2]{3,2,1,0:T(8,128)S(1)} %multiply_multiply_, ...), kind=kLoop, calls=%fused_computation.11 | loop fusion | flops 24576 | bytes 148480 | tf_op jit(solution)/shard_map/mul | solution.py:82
  69.3 2.5 copy.54
  71.9 2.5 copy.55
  74.4 2.5 copy.52
  76.9 2.5 copy.53
  79.5 0.8 add_convert_fusion.2
  80.2 0.8 subtract_convert_fusion.1
  81.6 2.0 copy.56
  83.6 2.1 convert_element_type.69
  85.7 14.5 %all_to_all.67 = bf16[2,4,768]{2,0,1:T(2,128)(2,1)} all-to-all(bf16[2,4,768]{2,0,1:T(2,128)(2,1)S(1)} %copy.57), channel_id=1, replica_groups=mesh['row'=8,'col'=4] {'col'}, dimensions={1} | all-to-all | bytes 24576 | tf_op jit(solution)/shard_map/all_to_all | solution.py:137
  100.3 0.7 all_to_all.60
  101.0 1.6 pad_maximum_fusion
  102.7 0.7 all-gather.7.cloned.1.call-update
  103.4 3.9 %all-to-all-start.1 = ((bf16[2,4,768]{2,0,1:T(2,128)(2,1)}), bf16[2,4,768]{2,0,1:T(2,128)(2,1)S(1)}, u32[]{:S(2)}, u32[]{:S(2)}) async-start(bf16[2,4,768]{2,0,1:T(2,128)(2,1)} %bitcast.72), calls=%async_computation.1 | async-start | bytes 24576 | tf_op jit(solution)/shard_map/all_to_all | solution.py:138
  107.9 2.6 all-to-all-done.1
  111.1 0.7 all_to_all.57
  112.4 1.6 constant_dynamic-update-slice_fusion
  114.2 1.4 select_reduce_fusion.1
  115.6 2.5 copy.61
  118.1 2.5 copy.62
  120.6 1.1 copy.59
  122.3 3.3 collective-permute-done
  125.6 0.8 add_convert_fusion.1
  126.4 4.2 %collective-permute-start.4 = (bf16[136,768]{1,0:T(8,128)(2,1)}, bf16[136,768]{1,0:T(8,128)(2,1)S(1)}, u32[]{:S(2)}, u32[]{:S(2)}) collective-permute-start(bf16[136,768]{1,0:T(8,128)(2,1)} %constant_dynamic-update-slice_fusion), channel_id=1, source_target_pairs={{0,28},{4,0},{8,4},{12,8},{16,12},{20,16},{24,20},{28,24},{1,29},{... | collective-permute-start | bytes 626696 | tf_op jit(solution)/shard_map/ppermute | solution.py:22
  130.6 4.2 %collective-permute-done.1 = bf16[136,768]{1,0:T(8,128)(2,1)S(1)} collective-permute-done((bf16[136,768]{1,0:T(8,128)(2,1)}, bf16[136,768]{1,0:T(8,128)(2,1)S(1)}, u32[]{:S(2)}, u32[]{:S(2)}) %collective-permute-start.1) | collective-permute-done | bytes 208928 | tf_op jit(solution)/shard_map/ppermute | solution.py:20
  134.8 1.0 collective-permute-start.2
  135.8 0.7 subtract_convert_fusion
  137.0 1.1 convert_element_type.71
  138.7 9.8 %all-to-all-start.3 = ((bf16[2,4,768]{2,0,1:T(2,128)(2,1)}), bf16[2,4,768]{2,0,1:T(2,128)(2,1)S(1)}, u32[]{:S(2)}, u32[]{:S(2)}) async-start(bf16[2,4,768]{2,0,1:T(2,128)(2,1)} %copy.64), calls=%async_computation.3 | async-start | bytes 24576 | tf_op jit(solution)/shard_map/all_to_all | solution.py:136
  148.5 2.0 collective-permute-start.5
  152.0 6.5 %collective-permute-done.5 = bf16[136,768]{1,0:T(8,128)(2,1)S(1)} collective-permute-done((bf16[136,768]{1,0:T(8,128)(2,1)S(1)}, bf16[136,768]{1,0:T(8,128)(2,1)S(1)}, u32[]{:S(2)}, u32[]{:S(2)}) %collective-permute-start.5) | collective-permute-done | bytes 208928 | tf_op jit(solution)/shard_map/ppermute | solution.py:22
  158.6 4.9 %collective-permute-start.6 = (bf16[136,768]{1,0:T(8,128)(2,1)S(1)}, bf16[136,768]{1,0:T(8,128)(2,1)S(1)}, u32[]{:S(2)}, u32[]{:S(2)}) collective-permute-start(bf16[136,768]{1,0:T(8,128)(2,1)S(1)} %collective-permute-done.5), channel_id=1, source_target_pairs={{0,28},{4,0},{8,4},{12,8},{16,12},{20,16},{24,20},{28,24},{1,29},{... | collective-permute-start | bytes 626696 | tf_op jit(solution)/shard_map/ppermute | solution.py:22
  163.5 0.9 constant_dynamic-update-slice_fusion.16
  164.6 2.3 collective-permute-done.6
  167.0 0.9 constant_dynamic-update-slice_fusion.7
  168.0 1.6 constant_dynamic-slice_fusion.4
  169.7 2.8 copy.51
  172.5 3.9 %copy.58 = bf16[1088,768]{0,1:T(8,128)(2,1)} copy(bf16[1088,768]{1,0:T(8,128)(2,1)} %all-gather.5.cloned.1.call-done) | data formatting | bytes 3342336 | tf_op jit(solution)/shard_map/all_gather | solution.py:147
  176.3 1.9 select_reduce_fusion
  178.4 65.5 %all-gather.7.cloned.1.call-done = bf16[768,3072]{1,0:T(8,128)(2,1)} async-done(((bf16[768,384]{1,0:T(8,128)(2,1)}), bf16[768,3072]{1,0:T(8,128)(2,1)}) %all-gather.7.cloned.1.call-update) | async-done | bytes 4718608 | tf_op jit(solution)/shard_map/all_gather | solution.py:185
  244.0 3.7 convolution_convert_fusion
  247.6 11.2 %all-reduce = bf16[8,3072]{1,0:T(8,128)(2,1)S(1)} all-reduce(bf16[8,3072]{1,0:T(8,128)(2,1)S(1)} %convolution_convert_fusion), channel_id=2, replica_groups=mesh['row'=8,'col'=4] {'col'}, use_global_device_ids=true, to_apply=%region_11.12.clone | all-reduce | flops 24576 | bytes 98304
  259.3 24.4 %all-gather.1 = bf16[8,2,3072]{2,1,0:T(2,128)(2,1)S(1)} all-gather(bf16[1,2,3072]{2,1,0:T(2,128)(2,1)S(1)} %fusion.51), channel_id=1, replica_groups=mesh['row'=8,'col'=4] {'row'}, dimensions={0}, use_global_device_ids=true | all-gather | bytes 110592 | tf_op jit(solution)/shard_map/all_gather | solution.py:192
  283.8 9.6 %fusion.22 = f32[16,3072]{1,0:T(8,128)} fusion(bf16[1536,3072]{1,0:T(8,128)(2,1)} %param.28, bf16[16,3072]{1,0:T(8,128)(2,1)S(1)} %reshape.272, bf16[3072,1536]{1,0:T(8,128)(2,1)} %param.27), kind=kOutput, calls=%fused_computation.36 | convolution fusion | flops 302211072 | bytes 19169280 | tf_op jit(solution)/shard_map/dot_general | solution.py:196
  294.7 71.4 %all-reduce.3.cloned.1.call-done = f32[16,3072]{1,0:T(8,128)} async-done(((f32[16,3072]{1,0:T(8,128)}), f32[16,3072]{1,0:T(8,128)}) %all-reduce.3.cloned.1.call-update) | async-done | bytes 196624 | tf_op jit(solution)/shard_map/psum | solution.py:197
  366.1 1.0 fusion.82
  367.7 5.6 %collective-permute-start.7 = (f32[1,64]{1,0:T(1,128)S(1)}, f32[1,64]{1,0:T(1,128)S(1)}, u32[]{:S(2)}, u32[]{:S(2)}) collective-permute-start(f32[1,64]{1,0:T(1,128)S(1)} %get-tuple-element.45), channel_id=1, source_target_pairs={{0,1},{1,2},{2,3},{4,5},{5,6},{6,7},{8,9},{9,10},{10,11},{12,13},{... | collective-permute-start | bytes 776 | tf_op jit(solution)/shard_map/ppermute | solution.py:35
  373.2 1.9 collective-permute-start.8
  375.2 2.9 collective-permute-done.8
  (113 shorter events, 12.2 us)
Async XLA Ops:
  7.2 360.2 %copy-start = (bf16[3072,64]{0,1:T(8,128)(2,1)S(1)}, bf16[3072,64]{0,1:T(8,128)(2,1)}, u32[]{:S(2)}) copy-start(bf16[3072,64]{0,1:T(8,128)(2,1)} %param.29) | copy-start | bytes 1179652
  41.0 9.8 %copy-start.12 = (s32[4,2]{0,1:T(2,128)S(1)}, s32[4,2]{0,1:T(2,128)}, u32[]{:S(2)}) copy-start(s32[4,2]{0,1:T(2,128)} %param.21) | copy-start | bytes 100
  41.0 9.8 %copy-start.13 = (s32[4,2]{0,1:T(2,128)S(1)}, s32[4,2]{0,1:T(2,128)}, u32[]{:S(2)}) copy-start(s32[4,2]{0,1:T(2,128)} %param.22) | copy-start | bytes 100
  41.0 12.2 %copy-start.15 = (f32[128]{0:T(128)S(1)}, f32[128]{0:T(128)}, u32[]{:S(2)}) copy-start(f32[128]{0:T(128)} %param.24) | copy-start | bytes 1540
  41.0 12.9 %copy-start.16 = (f32[128]{0:T(128)S(1)}, f32[128]{0:T(128)}, u32[]{:S(2)}) copy-start(f32[128]{0:T(128)} %param.25) | copy-start | bytes 1540
  45.7 10.6 %all-to-all-start = ((bf16[8,2,1152]{2,1,0:T(2,128)(2,1)}), bf16[8,2,1152]{2,1,0:T(2,128)(2,1)S(1)}, u32[]{:S(2)}, u32[]{:S(2)}) async-start(bf16[8,2,1152]{2,1,0:T(2,128)(2,1)} %all_to_all.50), calls=%async_computation | async-start | bytes 73728 | tf_op jit(solution)/shard_map/all_to_all | solution.py:127
  50.7 121.7 %all-gather.5.cloned.1.call-start = ((), (), s32[]{:S(2)}) async-start(), calls=%async_computation.4 | async-start | bytes 1880064 | tf_op jit(solution)/shard_map/all_gather | solution.py:147
  102.6 141.3 %all-gather.7.cloned.1.call-start = ((), (), s32[]{:S(2)}) async-start(), calls=%async_computation.5 | async-start | bytes 5308416 | tf_op jit(solution)/shard_map/all_gather | solution.py:185
  103.4 7.1 %all-to-all-start.1 = ((bf16[2,4,768]{2,0,1:T(2,128)(2,1)}), bf16[2,4,768]{2,0,1:T(2,128)(2,1)S(1)}, u32[]{:S(2)}, u32[]{:S(2)}) async-start(bf16[2,4,768]{2,0,1:T(2,128)(2,1)} %bitcast.72), calls=%async_computation.1 | async-start | bytes 24576 | tf_op jit(solution)/shard_map/all_to_all | solution.py:138
  110.5 0.6 copy-start.7
  114.0 11.6 %collective-permute-start = (bf16[136,768]{1,0:T(8,128)(2,1)}, bf16[136,768]{1,0:T(8,128)(2,1)}, u32[]{:S(2)}, u32[]{:S(2)}) collective-permute-start(bf16[136,768]{1,0:T(8,128)(2,1)} %constant_dynamic-update-slice_fusion), channel_id=1, source_target_pairs={{0,4},{4,8},{8,12},{12,16},{16,20},{20,24},{24,28},{28,0},{1,5},{5... | collective-permute-start | bytes 626696 | tf_op jit(solution)/shard_map/ppermute | solution.py:20
  118.1 32.5 %copy-start.17 = (u32[32]{0:T(128)S(1)}, u32[32]{0:T(128)}, u32[]{:S(2)}) copy-start(u32[32]{0:T(128)} %constant.178) | copy-start | bytes 388
  121.8 28.7 %copy-start.8 = (s32[1088]{0:T(1024)S(1)}, s32[1088]{0:T(1024)}, u32[]{:S(2)}) copy-start(s32[1088]{0:T(1024)} %get-tuple-element.2) | copy-start | bytes 13060
  121.8 28.7 %copy-start.9 = (s32[1088]{0:T(1024)S(1)}, s32[1088]{0:T(1024)}, u32[]{:S(2)}) copy-start(s32[1088]{0:T(1024)} %get-tuple-element.3) | copy-start | bytes 13060
  121.8 42.7 %copy-start.1 = (bf16[128,768]{1,0:T(8,128)(2,1)S(1)}, bf16[128,768]{1,0:T(8,128)(2,1)}, u32[]{:S(2)}) copy-start(bf16[128,768]{1,0:T(8,128)(2,1)} %param.18) | copy-start | bytes 589828
  125.6 9.2 %collective-permute-start.1 = (bf16[136,768]{1,0:T(8,128)(2,1)}, bf16[136,768]{1,0:T(8,128)(2,1)S(1)}, u32[]{:S(2)}, u32[]{:S(2)}) collective-permute-start(bf16[136,768]{1,0:T(8,128)(2,1)} %collective-permute-done), channel_id=1, source_target_pairs={{0,4},{4,8},{8,12},{12,16},{16,20},{20,24},{24,28},{28,0},{1,5},{5... | collective-permute-start | bytes 626696 | tf_op jit(solution)/shard_map/ppermute | solution.py:20
  126.4 22.1 %collective-permute-start.4 = (bf16[136,768]{1,0:T(8,128)(2,1)}, bf16[136,768]{1,0:T(8,128)(2,1)S(1)}, u32[]{:S(2)}, u32[]{:S(2)}) collective-permute-start(bf16[136,768]{1,0:T(8,128)(2,1)} %constant_dynamic-update-slice_fusion), channel_id=1, source_target_pairs={{0,28},{4,0},{8,4},{12,8},{16,12},{20,16},{24,20},{28,24},{1,29},{... | collective-permute-start | bytes 626696 | tf_op jit(solution)/shard_map/ppermute | solution.py:22
  134.8 15.7 %collective-permute-start.2 = (bf16[136,768]{1,0:T(8,128)(2,1)S(1)}, bf16[136,768]{1,0:T(8,128)(2,1)S(1)}, u32[]{:S(2)}, u32[]{:S(2)}) collective-permute-start(bf16[136,768]{1,0:T(8,128)(2,1)S(1)} %collective-permute-done.1), channel_id=1, source_target_pairs={{0,4},{4,8},{8,12},{12,16},{16,20},{20,24},{24,28},{28,0},{1,5},{5... | collective-permute-start | bytes 626696 | tf_op jit(solution)/shard_map/ppermute | solution.py:20
  138.7 13.3 %all-to-all-start.3 = ((bf16[2,4,768]{2,0,1:T(2,128)(2,1)}), bf16[2,4,768]{2,0,1:T(2,128)(2,1)S(1)}, u32[]{:S(2)}, u32[]{:S(2)}) async-start(bf16[2,4,768]{2,0,1:T(2,128)(2,1)} %copy.64), calls=%async_computation.3 | async-start | bytes 24576 | tf_op jit(solution)/shard_map/all_to_all | solution.py:136
  148.5 217.6 %all-reduce.3.cloned.1.call-start = ((), (), s32[]{:S(2)}) async-start(), calls=%async_computation.6 | async-start | bytes 393216 | tf_op jit(solution)/shard_map/psum | solution.py:197
  148.5 10.1 %collective-permute-start.5 = (bf16[136,768]{1,0:T(8,128)(2,1)S(1)}, bf16[136,768]{1,0:T(8,128)(2,1)S(1)}, u32[]{:S(2)}, u32[]{:S(2)}) collective-permute-start(bf16[136,768]{1,0:T(8,128)(2,1)S(1)} %collective-permute-done.4), channel_id=1, source_target_pairs={{0,28},{4,0},{8,4},{12,8},{16,12},{20,16},{24,20},{28,24},{1,29},{... | collective-permute-start | bytes 626696 | tf_op jit(solution)/shard_map/ppermute | solution.py:22
  150.5 13.0 %collective-permute-start.3 = (bf16[136,768]{1,0:T(8,128)(2,1)S(1)}, bf16[136,768]{1,0:T(8,128)(2,1)S(1)}, u32[]{:S(2)}, u32[]{:S(2)}) collective-permute-start(bf16[136,768]{1,0:T(8,128)(2,1)S(1)} %collective-permute-done.2), channel_id=1, source_target_pairs={{0,4},{4,8},{8,12},{12,16},{16,20},{20,24},{24,28},{28,0},{1,5},{5... | collective-permute-start | bytes 626696 | tf_op jit(solution)/shard_map/ppermute | solution.py:20
  158.6 8.3 %collective-permute-start.6 = (bf16[136,768]{1,0:T(8,128)(2,1)S(1)}, bf16[136,768]{1,0:T(8,128)(2,1)S(1)}, u32[]{:S(2)}, u32[]{:S(2)}) collective-permute-start(bf16[136,768]{1,0:T(8,128)(2,1)S(1)} %collective-permute-done.5), channel_id=1, source_target_pairs={{0,28},{4,0},{8,4},{12,8},{16,12},{20,16},{24,20},{28,24},{1,29},{... | collective-permute-start | bytes 626696 | tf_op jit(solution)/shard_map/ppermute | solution.py:22
  244.0 14.9 %copy-start.2 = (bf16[2,3072]{1,0:T(2,128)(2,1)S(1)}, bf16[2,3072]{1,0:T(2,128)(2,1)}, u32[]{:S(2)}) copy-start(bf16[2,3072]{1,0:T(2,128)(2,1)} %param.15) | copy-start | bytes 36868
  244.0 14.9 %copy-start.6 = (f32[1,1,3072]{2,1,0:T(1,128)S(1)}, f32[1,1,3072]{2,1,0:T(1,128)}, u32[]{:S(2)}) copy-start(f32[1,1,3072]{2,1,0:T(1,128)} %get-tuple-element.30) | copy-start | bytes 36868
  244.0 15.3 %copy-start.4 = (f32[1,1,3072]{2,1,0:T(1,128)S(1)}, f32[1,1,3072]{2,1,0:T(1,128)}, u32[]{:S(2)}) copy-start(f32[1,1,3072]{2,1,0:T(1,128)} %get-tuple-element.25) | copy-start | bytes 36868
  244.0 15.3 %copy-start.5 = (f32[1,1,3072]{2,1,0:T(1,128)S(1)}, f32[1,1,3072]{2,1,0:T(1,128)}, u32[]{:S(2)}) copy-start(f32[1,1,3072]{2,1,0:T(1,128)} %get-tuple-element.26) | copy-start | bytes 36868
  283.8 82.3 %copy-start.3 = (f32[1,1,3072]{2,1,0:T(1,128)S(1)}, f32[1,1,3072]{2,1,0:T(1,128)}, u32[]{:S(2)}) copy-start(f32[1,1,3072]{2,1,0:T(1,128)} %get-tuple-element.27) | copy-start | bytes 36868
  283.8 83.6 %copy-start.10 = (f32[1,1,3072]{2,1,0:T(1,128)S(1)}, f32[1,1,3072]{2,1,0:T(1,128)}, u32[]{:S(2)}) copy-start(f32[1,1,3072]{2,1,0:T(1,128)} %get-tuple-element.24) | copy-start | bytes 36868
  283.8 83.6 %copy-start.11 = (f32[1,1,3072]{2,1,0:T(1,128)S(1)}, f32[1,1,3072]{2,1,0:T(1,128)}, u32[]{:S(2)}) copy-start(f32[1,1,3072]{2,1,0:T(1,128)} %get-tuple-element.31) | copy-start | bytes 36868
  283.8 94.3 %copy-start.14 = (f32[2,64]{1,0:T(2,128)S(1)}, f32[2,64]{1,0:T(2,128)}, u32[]{:S(2)}) copy-start(f32[2,64]{1,0:T(2,128)} %param.16) | copy-start | bytes 1540
  367.7 7.5 %collective-permute-start.7 = (f32[1,64]{1,0:T(1,128)S(1)}, f32[1,64]{1,0:T(1,128)S(1)}, u32[]{:S(2)}, u32[]{:S(2)}) collective-permute-start(f32[1,64]{1,0:T(1,128)S(1)} %get-tuple-element.45), channel_id=1, source_target_pairs={{0,1},{1,2},{2,3},{4,5},{5,6},{6,7},{8,9},{9,10},{10,11},{12,13},{... | collective-permute-start | bytes 776 | tf_op jit(solution)/shard_map/ppermute | solution.py:35
  373.2 4.9 %collective-permute-start.8 = (f32[1,64]{1,0:T(1,128)S(1)}, f32[1,64]{1,0:T(1,128)S(1)}, u32[]{:S(2)}, u32[]{:S(2)}) collective-permute-start(f32[1,64]{1,0:T(1,128)S(1)} %get-tuple-element.46), channel_id=1, source_target_pairs={{1,0},{2,1},{3,2},{5,4},{6,5},{7,6},{9,8},{10,9},{11,10},{13,12},{... | collective-permute-start | bytes 776 | tf_op jit(solution)/shard_map/ppermute | solution.py:37
Sparse Core Ops, SparseCore 0:
  102.8 58.0 all-gather.4
  162.9 81.0 all-gather.6
  293.6 72.4 all-reduce.2
